TPU v7x, 32 devices: a whole 2x2x4 slice. The times are simulated.
32 devices in a mesh: dp: 8 (over y, x, core), tensor: 4 (over z).
Axes of the slice: x: 2, y: 2, z: 4, core: 2. Of those that a mesh axis runs over, the one named last changes fastest.
Arguments:
- layer_input: bfloat16 [32768, 768], P('dp'), may hold values from -6 to 6
- segments: int32 [32, 1024], P('dp'), may hold values from 0 to 7, never falling along the last dimension, each value on 1 to 512 neighbouring positions
- query_weight: bfloat16 [768, 768], P(None, 'tensor'), may hold values from -0.21875 to 0.21875
- query_bias: float32 [768], P('tensor'), may hold values from -3 to 3
- key_weight: bfloat16 [768, 768], P(None, 'tensor'), may hold values from -0.21875 to 0.21875
- value_weight: bfloat16 [768, 768], P(None, 'tensor'), may hold values from -0.21875 to 0.21875
- value_bias: float32 [768], P('tensor'), may hold values from -3 to 3
- output_weight: bfloat16 [768, 768], P('tensor'), may hold values from -0.875 to 0.875
- output_bias: float32 [768], replicated, may hold values from -3 to 3
- first_gain: float32 [768], replicated, may hold values from 0.5 to 1.5
- first_shift: float32 [768], replicated, may hold values from -3 to 3
- up_weight: bfloat16 [768, 3072], P(None, 'tensor'), may hold values from -0.21875 to 0.21875
- up_bias: float32 [3072], P('tensor'), may hold values from -3 to 3
- down_weight: bfloat16 [3072, 768], P('tensor'), may hold values from -0.109375 to 0.109375
- down_bias: float32 [768], replicated, may hold values from -3 to 3
- second_gain: float32 [768], replicated, may hold values from 0.5 to 1.5
- second_shift: float32 [768], replicated, may hold values from -3 to 3
- output_grad: bfloat16 [32768, 768], P('dp'), may hold values from -6 to 6
Outputs:
- layer_output: bfloat16 [32768, 768], P(('dp', 'tensor'))
- input_grad: float32 [32768, 768], P(('dp', 'tensor'))
- grad_query_weight: float32 [768, 768], P('dp', 'tensor')
- grad_query_bias: float32 [768], P('tensor')
- grad_key_weight: float32 [768, 768], P('dp', 'tensor')
- grad_value_weight: float32 [768, 768], P('dp', 'tensor')
- grad_value_bias: float32 [768], P('tensor')
- grad_output_weight: float32 [768, 768], P('tensor', 'dp')
- grad_output_bias: float32 [768], P(('dp', 'tensor'))
- grad_first_gain: float32 [768], P(('dp', 'tensor'))
- grad_first_shift: float32 [768], P(('dp', 'tensor'))
- grad_up_weight: float32 [768, 3072], P('dp', 'tensor')
- grad_up_bias: float32 [3072], P('tensor')
- grad_down_weight: float32 [3072, 768], P('tensor', 'dp')
- grad_down_bias: float32 [768], P(('dp', 'tensor'))
- grad_second_gain: float32 [768], P(('dp', 'tensor'))
- grad_second_shift: float32 [768], P(('dp', 'tensor'))
Inputs may be any that keep to these rules, and one draw needn't show every extreme that they name: `segments`: segment numbers restart in every packed row; a token attends exactly to the tokens of its own row that carry its segment number.
All inputs are finite; a program needn't handle non-finite values.
Results may differ from a plain program's by a relative error of at most 0.02.
The roundings to bfloat16 on the way count: a program that leaves them out, or rounds other values in their place, can miss the bound.
Values may be sent and summed in bfloat16 or wider, within the bound.
A program may use at most 256 MiB of HBM per device.

v0:
```python
import jax
import jax.numpy as jnp
from jax import lax
from jax.sharding import PartitionSpec as P

HEAD_DIM = 64
norm_eps = 1e-06


def product(left_side, right_side):
    return jnp.dot(left_side, right_side, preferred_element_type=jnp.float32)


def contract_rows(left_side, right_side):
    return lax.dot_general(
        left_side, right_side, (((0,), (0,)), ((), ())), preferred_element_type=jnp.float32
    )


def contract_last(left_side, right_side):
    return lax.dot_general(
        left_side, right_side, (((1,), (1,)), ((), ())), preferred_element_type=jnp.float32
    )


def normalize(summed, norm_gain, offset):
    centred = summed - jnp.mean(summed, -1, keepdims=True)
    inverse = lax.rsqrt(jnp.mean(centred * centred, -1, keepdims=True) + norm_eps)
    scaled = centred * inverse
    return (scaled * norm_gain + offset, scaled, inverse)


def normalize_back(grad_out, scaled, inverse, norm_gain):
    grad_scaled = grad_out * norm_gain
    mean_grad = jnp.mean(grad_scaled, -1, keepdims=True)
    mean_cross = jnp.mean(grad_scaled * scaled, -1, keepdims=True)
    return inverse * (grad_scaled - mean_grad - scaled * mean_cross)


def gelu_tanh(pre_act):
    return jax.nn.gelu(pre_act, approximate=True)


def score_block(query_block, key_row, query_segment, key_segment):
    scores = jnp.einsum(
        "qhd,khd->hqk", query_block, key_row, preferred_element_type=jnp.float32
    ) * HEAD_DIM ** (-0.5)
    linked = query_segment[:, None] == key_segment[None, :]
    return jnp.where(linked[None], scores, -1e30)


def attend(queries, key_side, value_proj, segments, block_rows):
    row_count, row_len = segments.shape
    head_count = queries.shape[1] // HEAD_DIM
    key_rows = key_side.reshape(row_count, row_len, head_count, HEAD_DIM)
    value_rows = value_proj.reshape(row_count, row_len, head_count, HEAD_DIM)
    block_count = row_count * row_len // block_rows
    query_blocks = queries.reshape(block_count, block_rows, head_count, HEAD_DIM)
    segment_blocks = segments.reshape(block_count, block_rows)
    row_ids = jnp.arange(block_count, dtype=jnp.int32) // (row_len // block_rows)

    def one_block(inputs):
        query_block, query_segment, row_id = inputs
        scores = score_block(query_block, key_rows[row_id], query_segment, segments[row_id])
        row_max = jnp.max(scores, -1, keepdims=True)
        exp_scores = jnp.exp(scores - row_max)
        row_total = jnp.sum(exp_scores, -1, keepdims=True)
        prob_low = (exp_scores / row_total).astype(jnp.bfloat16)
        context = jnp.einsum(
            "hqk,khd->qhd", prob_low, value_rows[row_id], preferred_element_type=jnp.float32
        )
        return (context.astype(jnp.bfloat16), (row_max + jnp.log(row_total))[..., 0])

    context, log_total = lax.map(one_block, (query_blocks, segment_blocks, row_ids))
    return (context.reshape(row_count * row_len, head_count * HEAD_DIM), log_total)


def attend_back(queries, key_side, value_proj, segments, log_total, grad_context, block_rows):
    row_count, row_len = segments.shape
    head_count = queries.shape[1] // HEAD_DIM
    local_width = head_count * HEAD_DIM
    key_rows = key_side.reshape(row_count, row_len, head_count, HEAD_DIM)
    value_rows = value_proj.reshape(row_count, row_len, head_count, HEAD_DIM)
    block_count = row_count * row_len // block_rows
    per_row = row_len // block_rows
    query_blocks = queries.reshape(block_count, block_rows, head_count, HEAD_DIM)
    grad_blocks = grad_context.reshape(block_count, block_rows, head_count, HEAD_DIM)
    segment_blocks = segments.reshape(block_count, block_rows)
    row_ids = jnp.arange(block_count, dtype=jnp.int32) // per_row

    def one_block(inputs):
        query_block, query_segment, row_id, log_block, grad_block = inputs
        scores = score_block(query_block, key_rows[row_id], query_segment, segments[row_id])
        probs_full = jnp.exp(scores - log_block[..., None])
        grad_probs = jnp.einsum(
            "qhd,khd->hqk", grad_block, value_rows[row_id], preferred_element_type=jnp.float32
        )
        inner_sum = jnp.sum(probs_full * grad_probs, -1, keepdims=True)
        grad_scores = (probs_full * (grad_probs - inner_sum)).astype(jnp.bfloat16)
        grad_query = jnp.einsum(
            "hqk,khd->qhd", grad_scores, key_rows[row_id], preferred_element_type=jnp.float32
        ) * HEAD_DIM ** (-0.5)
        grad_key = jnp.einsum(
            "hqk,qhd->khd", grad_scores, query_block, preferred_element_type=jnp.float32
        ) * HEAD_DIM ** (-0.5)
        grad_value = jnp.einsum(
            "hqk,qhd->khd",
            probs_full.astype(jnp.bfloat16),
            grad_block,
            preferred_element_type=jnp.float32,
        )
        return (grad_query, grad_key, grad_value)

    grad_query, grad_key, grad_value = lax.map(
        one_block, (query_blocks, segment_blocks, row_ids, log_total, grad_blocks)
    )
    grad_query = grad_query.reshape(row_count * row_len, local_width)
    grad_key = (
        grad_key.reshape(row_count, per_row, row_len, local_width)
        .sum(1)
        .reshape(row_count * row_len, local_width)
    )
    grad_value = (
        grad_value.reshape(row_count, per_row, row_len, local_width)
        .sum(1)
        .reshape(row_count * row_len, local_width)
    )
    return (grad_query, grad_key, grad_value)


def on_device(
    layer_input,
    segments,
    query_weight,
    query_bias,
    key_weight,
    value_weight,
    value_bias,
    output_weight,
    output_bias,
    first_gain,
    first_shift,
    up_weight,
    up_bias,
    down_weight,
    down_bias,
    second_gain,
    second_shift,
    output_grad,
):
    part_count = lax.axis_size("tensor")
    part_id = lax.axis_index("tensor")
    tok_count = layer_input.shape[0]
    share_rows = tok_count // part_count
    block_rows = min(512, segments.shape[1])

    def own_rows(full_array):
        return lax.dynamic_slice_in_dim(full_array, part_id * share_rows, share_rows, 0)

    input_f32 = layer_input.astype(jnp.float32)
    queries = (product(layer_input, query_weight) + query_bias).astype(jnp.bfloat16)
    key_side = product(layer_input, key_weight).astype(jnp.bfloat16)
    value_proj = (product(layer_input, value_weight) + value_bias).astype(jnp.bfloat16)
    context, log_total = attend(queries, key_side, value_proj, segments, block_rows)
    attn_total = lax.psum(product(context, output_weight).astype(jnp.bfloat16), "tensor").astype(
        jnp.float32
    )
    first_in = input_f32 + attn_total + output_bias
    first_out, first_unit, first_inv = normalize(first_in, first_gain, first_shift)
    first_low = first_out.astype(jnp.bfloat16)
    first_mine = own_rows(first_out)
    pre_act = product(first_low, up_weight) + up_bias
    gelu_out, pull_gelu = jax.vjp(gelu_tanh, pre_act)
    hidden_low = gelu_out.astype(jnp.bfloat16)
    down_mine = lax.psum_scatter(
        product(hidden_low, down_weight).astype(jnp.bfloat16),
        "tensor",
        scatter_dimension=0,
        tiled=True,
    ).astype(jnp.float32)
    second_in = first_mine + down_mine + down_bias
    second_out, second_unit, second_inv = normalize(second_in, second_gain, second_shift)
    layer_output = second_out.astype(jnp.bfloat16)
    grad_out_mine = own_rows(output_grad).astype(jnp.float32)
    grad_second = normalize_back(grad_out_mine, second_unit, second_inv, second_gain)
    grad_second_gain = jnp.sum(grad_out_mine * second_unit, 0)
    grad_second_shift = jnp.sum(grad_out_mine, 0)
    grad_down_bias = jnp.sum(grad_second, 0)
    down_low = lax.all_gather(grad_second.astype(jnp.bfloat16), "tensor", axis=0, tiled=True)
    grad_down_weight = contract_rows(hidden_low, down_low)
    grad_hidden = contract_last(down_low, down_weight)
    grad_pre = pull_gelu(grad_hidden)[0].astype(jnp.bfloat16)
    grad_up_weight = contract_rows(first_low, grad_pre)
    grad_up_bias = jnp.sum(grad_pre, 0, dtype=jnp.float32)
    up_back = contract_last(grad_pre, up_weight)
    mine_rows = own_rows(up_back) + grad_second
    first_grad = lax.psum(
        lax.dynamic_update_slice_in_dim(up_back, mine_rows, part_id * share_rows, 0).astype(
            jnp.bfloat16
        ),
        "tensor",
    ).astype(jnp.float32)
    attn_grad = normalize_back(first_grad, first_unit, first_inv, first_gain)
    attn_grad_low = attn_grad.astype(jnp.bfloat16)
    attn_grad_mine = own_rows(attn_grad)
    first_grad_mine = own_rows(first_grad)
    unit_mine = own_rows(first_unit)
    grad_first_gain = jnp.sum(first_grad_mine * unit_mine, 0)
    grad_first_shift = jnp.sum(first_grad_mine, 0)
    grad_output_bias = jnp.sum(attn_grad_mine, 0)
    grad_output_weight = contract_rows(context, attn_grad_low)
    grad_context = contract_last(attn_grad_low, output_weight).astype(jnp.bfloat16)
    grad_query, grad_key, grad_value = attend_back(
        queries, key_side, value_proj, segments, log_total, grad_context, block_rows
    )
    query_low = grad_query.astype(jnp.bfloat16)
    key_low = grad_key.astype(jnp.bfloat16)
    value_low = grad_value.astype(jnp.bfloat16)
    grad_query_weight = contract_rows(layer_input, query_low)
    grad_key_weight = contract_rows(layer_input, key_low)
    grad_value_weight = contract_rows(layer_input, value_low)
    grad_query_bias = jnp.sum(query_low, 0, dtype=jnp.float32)
    grad_value_bias = jnp.sum(value_low, 0, dtype=jnp.float32)
    total = contract_last(query_low, query_weight)
    total = total + contract_last(key_low, key_weight)
    input_grad = (
        lax.psum_scatter(
            (total + contract_last(value_low, value_weight)).astype(jnp.bfloat16),
            "tensor",
            scatter_dimension=0,
            tiled=True,
        ).astype(jnp.float32)
        + attn_grad_mine
    )
    summed_weights = (
        lax.psum_scatter(grad_query_weight, "dp", scatter_dimension=0, tiled=True),
        lax.psum_scatter(grad_key_weight, "dp", scatter_dimension=0, tiled=True),
        lax.psum_scatter(grad_value_weight, "dp", scatter_dimension=0, tiled=True),
        lax.psum_scatter(grad_up_weight, "dp", scatter_dimension=0, tiled=True),
        lax.psum_scatter(grad_output_weight, "dp", scatter_dimension=1, tiled=True),
        lax.psum_scatter(grad_down_weight, "dp", scatter_dimension=1, tiled=True),
    )
    summed_shared = (
        lax.psum_scatter(grad_output_bias, ("dp", "tensor"), scatter_dimension=0, tiled=True),
        lax.psum_scatter(grad_first_gain, ("dp", "tensor"), scatter_dimension=0, tiled=True),
        lax.psum_scatter(grad_first_shift, ("dp", "tensor"), scatter_dimension=0, tiled=True),
        lax.psum_scatter(grad_down_bias, ("dp", "tensor"), scatter_dimension=0, tiled=True),
        lax.psum_scatter(grad_second_gain, ("dp", "tensor"), scatter_dimension=0, tiled=True),
        lax.psum_scatter(grad_second_shift, ("dp", "tensor"), scatter_dimension=0, tiled=True),
    )
    summed_biases = lax.psum((grad_query_bias, grad_value_bias, grad_up_bias), "dp")
    return (
        layer_output,
        input_grad,
        summed_weights[0],
        summed_biases[0],
        summed_weights[1],
        summed_weights[2],
        summed_biases[1],
        summed_weights[4],
        summed_shared[0],
        summed_shared[1],
        summed_shared[2],
        summed_weights[3],
        summed_biases[2],
        summed_weights[5],
        summed_shared[3],
        summed_shared[4],
        summed_shared[5],
    )


def solution(mesh):
    in_specs = (
        P("dp", None),
        P("dp", None),
        P(None, "tensor"),
        P("tensor"),
        P(None, "tensor"),
        P(None, "tensor"),
        P("tensor"),
        P("tensor", None),
        P(),
        P(),
        P(),
        P(None, "tensor"),
        P("tensor"),
        P("tensor", None),
        P(),
        P(),
        P(),
        P("dp", None),
    )
    out_specs = (
        P(("dp", "tensor"), None),
        P(("dp", "tensor"), None),
        P("dp", "tensor"),
        P("tensor"),
        P("dp", "tensor"),
        P("dp", "tensor"),
        P("tensor"),
        P("tensor", "dp"),
        P(("dp", "tensor")),
        P(("dp", "tensor")),
        P(("dp", "tensor")),
        P("dp", "tensor"),
        P("tensor"),
        P("tensor", "dp"),
        P(("dp", "tensor")),
        P(("dp", "tensor")),
        P(("dp", "tensor")),
    )
    return jax.shard_map(
        on_device, mesh=mesh, in_specs=in_specs, out_specs=out_specs, check_vma=False
    )
```

profile of v0, /device:TPU:0, one launch (start us, length us, event | category | flops | bytes accessed | tf_op | source)
XLA Modules:
  0.0 1443.7 jit_solution(3081273717691375530)
XLA Ops:
  33.3 86.0 %while.26 = (s32[]{:T(128)}, bf16[8,512,3,64]{1,3,2,0:T(8,128)(2,1)}, f32[8,3,512]{2,1,0:T(4,128)S(1)}, s32[8]{0:T(128)S(1)}, bf16[4,1024,3,64]{1,3,2,0:T(8,128)...) while((s32[]{:T(128)}, ...), condition=%wide.region_3.4_spmd, body=%wide.region_0.3_spmd.sunk | while | flops 422148608 | bytes 22225096 | solution.py:74
  128.7 225.5 %all-reduce.11.cloned.1.call-done = bf16[4096,768]{1,0:T(8,128)(2,1)} async-done(((bf16[4096,768]{1,0:T(8,128)(2,1)}), bf16[4096,768]{1,0:T(8,128)(2,1)}) %all-reduce.11.cloned.1.call-update) | async-done | bytes 6291472 | tf_op jit(solution)/shard_map/psum | solution.py:165
  373.4 11.8 multiply_convert_fusion.1
  385.2 9.7 convolution_convert_fusion.1
  395.2 109.5 %reduce-scatter.17.cloned.1.call-done = bf16[1024,768]{1,0:T(8,128)(2,1)} async-done(((bf16[4096,768]{1,0:T(8,128)(2,1)}), bf16[1024,768]{1,0:T(8,128)(2,1)}) %reduce-scatter.17.cloned.1.call-update) | async-done | bytes 1572880 | tf_op jit(solution)/shard_map/reduce_scatter | solution.py:175
  518.5 116.0 %all-gather.2.cloned.1.call-done = bf16[4096,768]{1,0:T(8,128)(2,1)} async-done(((bf16[1024,768]{1,0:T(8,128)(2,1)}), bf16[4096,768]{1,0:T(8,128)(2,1)}) %all-gather.2.cloned.1.call-update) | async-done | bytes 6291472 | tf_op jit(solution)/shard_map/all_gather | solution.py:189
  634.5 16.9 %convert_reduce_fusion = (f32[768]{0:T(1024)}, bf16[4096,768]{1,0:T(8,128)(2,1)S(1)}) fusion(f32[4096,768]{1,0:T(8,128)} %get-tuple-element.361, f32[768]{0:T(1024)S(1)} %copy-done.34, bf16[4096,768]{1,0:T(8,128)(2,1)} %all-gather.2.cloned.1.call-done, bf16[768,768]{1,0:T(8,128)(2,1)S(1)} %copy-done.33), kind=kOutput, calls=%fused_computation.74 | convolution fusion | flops 4904188928 | bytes 26351616 | tf_op jit(solution)/shard_map/dot_general | solution.py:21
  651.5 8.3 fusion.85
  672.2 220.8 %all-reduce.13.cloned.1.call-done = bf16[4096,768]{1,0:T(8,128)(2,1)} async-done(((bf16[4096,768]{1,0:T(8,128)(2,1)}), bf16[4096,768]{1,0:T(8,128)(2,1)}) %all-reduce.13.cloned.1.call-update) | async-done | bytes 6291472 | tf_op jit(solution)/shard_map/psum | solution.py:197
  893.0 8.8 multiply_reduce_fusion.3
  901.8 7.9 subtract_multiply_fusion
  917.7 7.9 convolution_convert_fusion.2
  929.9 146.9 %while.27 = (s32[]{:T(128)}, bf16[8,512,3,64]{1,3,2,0:T(8,128)(2,1)}, f32[8,1024,3,64]{1,3,2,0:T(8,128)}, f32[8,1024,3,64]{1,3,2,0:T(8,128)}, s32[8]{0:T(128)S(1...) while((s32[]{:T(128)}, ...), condition=%wide.region_17.18_spmd, body=%wide.region_15.17_spmd.sunk | while | flops 1031043584 | bytes 53278952 | solution.py:114
  1103.9 12.8 add_convert_fusion
  1116.8 11.4 fusion.74
  1128.3 10.1 fusion.88
  1158.0 8.3 convert_element_type.121
  1166.6 15.1 %all-reduce.7 = (f32[192]{0:T(256)}, f32[192]{0:T(256)}, f32[768]{0:T(1024)}) all-reduce(f32[192]{0:T(256)S(1)} %reduce_sum.202, f32[192]{0:T(256)S(1)} %convert_reduce_fusion.2, f32[768]{0:T(1024)S(1)} %copy-done.32), channel_id=1, replica_groups=mesh['dp'=8,'tensor'=4] {'dp'}, use_global_device_ids=true, to_apply=%region_23.24 | all-reduce | flops 1152 | bytes 9216 | tf_op jit(solution)/shard_map/psum | solution.py:251
  1186.7 40.0 %reduce-scatter.19.cloned.1.call-done = bf16[1024,768]{1,0:T(8,128)(2,1)} async-done(((bf16[4096,768]{1,0:T(8,128)(2,1)}), bf16[1024,768]{1,0:T(8,128)(2,1)}) %reduce-scatter.19.cloned.1.call-update) | async-done | bytes 1572880 | tf_op jit(solution)/shard_map/reduce_scatter | solution.py:227
  1231.0 41.2 %all-reduce.6 = (f32[768]{0:T(1024)S(1)}, f32[768]{0:T(1024)S(1)}, f32[768]{0:T(1024)S(1)}, f32[768]{0:T(1024)S(1)}, f32[768]{0:T(1024)S(1)}, /*index=5*/f32[768]{0:T(1024)S(1)}) all-reduce(f32[768]{0:T(1024)S(1)} %get-tuple-element.357, f32[768]{0:T(1024)S(1)} %get-tuple-element.287, ...), channel_id=8, replica_groups=mesh['dp'=8,'tensor'=4] {'dp','tensor'}, use_global_device_ids=true, to_apply=%region_30.31.clone | all-reduce | flops 4608 | bytes 36864
  1275.7 45.1 %reduce-scatter.23.cloned.1.call-done = f32[768,96]{0,1:T(8,128)} async-done(((f32[768,768]{0,1:T(8,128)}), f32[768,96]{0,1:T(8,128)}) %reduce-scatter.23.cloned.1.call-update) | async-done | bytes 294928 | tf_op jit(solution)/shard_map/reduce_scatter | solution.py:241
  1320.8 38.8 %reduce-scatter.25.cloned.1.call-done = f32[96,192]{1,0:T(8,128)} async-done(((f32[768,192]{1,0:T(8,128)}), f32[96,192]{1,0:T(8,128)}) %reduce-scatter.25.cloned.1.call-update) | async-done | bytes 73744
  1359.6 38.6 %reduce-scatter.27.cloned.1.call-done = f32[96,192]{1,0:T(8,128)} async-done(((f32[768,192]{1,0:T(8,128)}), f32[96,192]{1,0:T(8,128)}) %reduce-scatter.27.cloned.1.call-update) | async-done | bytes 73744
  1398.1 38.8 %reduce-scatter.29.cloned.1.call-done = f32[96,192]{1,0:T(8,128)} async-done(((f32[768,192]{1,0:T(8,128)}), f32[96,192]{1,0:T(8,128)}) %reduce-scatter.29.cloned.1.call-update) | async-done | bytes 73744
  (323 shorter events, 353.8 us)
Async XLA Ops:
  7.2 366.2 %copy-start = (bf16[768,768]{1,0:T(8,128)(2,1)S(1)}, bf16[768,768]{1,0:T(8,128)(2,1)}, u32[]{:S(2)}) copy-start(bf16[768,768]{1,0:T(8,128)(2,1)} %param.33) | copy-start | bytes 3538948
  7.2 347.0 %all-reduce.11.cloned.1.call-start = ((), (), s32[]{:S(2)}) async-start(), calls=%async_computation.8 | async-start | bytes 12582912 | tf_op jit(solution)/shard_map/psum | solution.py:165
  123.9 230.3 %copy-start.23 = (f32[768]{0:T(1024)S(1)}, f32[768]{0:T(1024)}, u32[]{:S(2)}) copy-start(f32[768]{0:T(1024)} %param.30) | copy-start | bytes 9220
  128.5 376.2 %reduce-scatter.17.cloned.1.call-start = ((), (), s32[]{:S(2)}) async-start(), calls=%async_computation.9 | async-start | bytes 7864320 | tf_op jit(solution)/shard_map/reduce_scatter | solution.py:175
  354.2 13.0 slice-start.2
  373.4 11.8 copy-start.3
  394.9 109.9 %copy-start.31 = (f32[768]{0:T(1024)S(1)}, f32[768]{0:T(1024)}, u32[]{:S(2)}) copy-start(f32[768]{0:T(1024)} %param.36) | copy-start | bytes 9220
  394.9 113.2 %copy-start.26 = (f32[768]{0:T(1024)S(1)}, f32[768]{0:T(1024)}, u32[]{:S(2)}) copy-start(f32[768]{0:T(1024)} %param.37) | copy-start | bytes 9220
  394.9 239.6 %all-gather.2.cloned.1.call-start = ((), (), s32[]{:S(2)}) async-start(), calls=%async_computation.10 | async-start | bytes 7864320 | tf_op jit(solution)/shard_map/all_gather | solution.py:189
  395.2 116.3 %copy-start.29 = (f32[768]{0:T(1024)S(1)}, f32[768]{0:T(1024)}, u32[]{:S(2)}) copy-start(f32[768]{0:T(1024)} %param.38) | copy-start | bytes 9220
  518.5 374.5 %all-reduce.13.cloned.1.call-start = ((), (), s32[]{:S(2)}) async-start(), calls=%async_computation.11 | async-start | bytes 12582912 | tf_op jit(solution)/shard_map/psum | solution.py:197
  671.8 513.2 %reduce-scatter.31.cloned.1.call-start = ((), (), s32[]{:S(2)}) async-start(), calls=%async_computation.18 | async-start | bytes 884736
  901.8 12.5 copy-start.12
  925.7 301.0 %reduce-scatter.19.cloned.1.call-start = ((), (), s32[]{:S(2)}) async-start(), calls=%async_computation.12 | async-start | bytes 7864320 | tf_op jit(solution)/shard_map/reduce_scatter | solution.py:227
  1091.2 12.7 copy-start.15
  1116.8 158.9 %reduce-scatter.21.cloned.1.call-start = ((), (), s32[]{:S(2)}) async-start(), calls=%async_computation.13 | async-start | bytes 2654208 | tf_op jit(solution)/shard_map/reduce_scatter | solution.py:239
  1128.3 192.5 %reduce-scatter.23.cloned.1.call-start = ((), (), s32[]{:S(2)}) async-start(), calls=%async_computation.14 | async-start | bytes 2654208 | tf_op jit(solution)/shard_map/reduce_scatter | solution.py:241
  1138.4 221.1 %reduce-scatter.25.cloned.1.call-start = ((), (), s32[]{:S(2)}) async-start(), calls=%async_computation.15 | async-start | bytes 884736
  1144.3 253.8 %reduce-scatter.27.cloned.1.call-start = ((), (), s32[]{:S(2)}) async-start(), calls=%async_computation.16 | async-start | bytes 884736
  1150.2 286.7 %reduce-scatter.29.cloned.1.call-start = ((), (), s32[]{:S(2)}) async-start(), calls=%async_computation.17 | async-start | bytes 884736
  1166.6 270.3 %copy-start.1 = (bf16[768,768]{1,0:T(8,128)(2,1)S(1)}, bf16[768,768]{1,0:T(8,128)(2,1)}, u32[]{:S(2)}) copy-start(bf16[768,768]{1,0:T(8,128)(2,1)} %param.33) | copy-start | bytes 3538948
  1181.7 49.3 %copy-start.25 = (f32[768]{0:T(1024)S(1)}, f32[768]{0:T(1024)}, u32[]{:S(2)}) copy-start(f32[768]{0:T(1024)} %get-tuple-element.345) | copy-start | bytes 9220
  1181.7 49.3 %copy-start.27 = (f32[768]{0:T(1024)S(1)}, f32[768]{0:T(1024)}, u32[]{:S(2)}) copy-start(f32[768]{0:T(1024)} %get-tuple-element.288) | copy-start | bytes 9220
  1181.7 49.3 %copy-start.28 = (f32[768]{0:T(1024)S(1)}, f32[768]{0:T(1024)}, u32[]{:S(2)}) copy-start(f32[768]{0:T(1024)} %get-tuple-element.293) | copy-start | bytes 9220
  (27 other events, 180.1 us)
Sparse Core Ops, SparseCore 0:
  128.6 225.5 all-reduce.10
  395.0 109.6 reduce-scatter.16
  518.6 115.8 all-gather.1
  671.9 220.9 all-reduce.12
  925.8 33.9 reduce-scatter.30
  1116.9 109.6 reduce-scatter.18
  1230.6 43.4 reduce-scatter.20
  1278.3 42.4 reduce-scatter.22
  1324.5 34.9 reduce-scatter.24
  1363.1 34.9 reduce-scatter.26
  1401.9 34.9 reduce-scatter.28
where the time goes:
time: 1450 us; the launch traced here: 1440 us
  waiting for transfers between devices  873 us (60%)
  matrix products  294 us (20%)
  other arithmetic  121 us (8%)
  blocking collectives  56.3 us (4%)
  local copies, waits for them, and re-layouts  50.9 us (4%)
  loops' own time  31.9 us (2%)
  between operations  14.7 us (1%)
    psum x1, waiting for transfers between devices, on_device(): lax.psum(product(context, output_weight).astype(jnp.bfloat16), 'tensor')  225 us
    psum x1, waiting for transfers between devices, on_device(): lax.psum(lax.dynamic_update_slice_in_dim(up_back, mine_rows, part_id * sh...  221 us
    unnamed x15, waiting for transfers between devices  116 us
    all_gather x1, waiting for transfers between devices, on_device(): lax.all_gather(grad_second.astype(jnp.bfloat16), 'tensor', axis=0, tiled=...  116 us
    reduce_scatter x1, waiting for transfers between devices, on_device(): lax.psum_scatter(product(hidden_low, down_weight).astype(jnp.bfloat16), '...  110 us
    dot_general x6, matrix products, contract_last(): lax.dot_general(left_side, right_side, (((1,), (1,)), ((), ())), preferre...  58.7 us
    reduce_scatter x1, waiting for transfers between devices, on_device(): lax.psum_scatter(grad_down_weight, 'dp', scatter_dimension=1, tiled=True)  45.1 us
    unnamed x1, blocking collectives  41.2 us
  transfers between devices with their start and end apart: 11, of which 9 were waited for; matrix products, arithmetic and copies ran while one was open for 16% of the time, Pallas kernels for 0%

commit v1 on v0

--- a/solution.py
+++ b/solution.py
@@ -2,6 +2,7 @@
 import jax.numpy as jnp
 from jax import lax
 from jax.sharding import PartitionSpec as P
+from jax.lax import axis_index, ppermute, psum
 
 HEAD_DIM = 64
 norm_eps = 1e-06
@@ -148,6 +149,25 @@
     second_shift,
     output_grad,
 ):
+
+    def connect_thing_in(state):
+        after = psum(1, "tensor")
+        current_value = axis_index("tensor")
+        g_now, left_arr, heard = (after, current_value, state.shape[0])
+        seen_now, w_next = (state, 1)
+        while w_next < g_now:
+            seen_now = jnp.concatenate(
+                [
+                    seen_now,
+                    ppermute(
+                        seen_now, "tensor", tuple(((c, (c - w_next) % g_now) for c in range(g_now)))
+                    ),
+                ],
+                0,
+            )
+            w_next = 2 * w_next
+        return jnp.roll(seen_now, left_arr * heard, 0)
+
     part_count = lax.axis_size("tensor")
     part_id = lax.axis_index("tensor")
     tok_count = layer_input.shape[0]
@@ -186,7 +206,7 @@
     grad_second_gain = jnp.sum(grad_out_mine * second_unit, 0)
     grad_second_shift = jnp.sum(grad_out_mine, 0)
     grad_down_bias = jnp.sum(grad_second, 0)
-    down_low = lax.all_gather(grad_second.astype(jnp.bfloat16), "tensor", axis=0, tiled=True)
+    down_low = connect_thing_in(grad_second.astype(jnp.bfloat16))
     grad_down_weight = contract_rows(hidden_low, down_low)
     grad_hidden = contract_last(down_low, down_weight)
     grad_pre = pull_gelu(grad_hidden)[0].astype(jnp.bfloat16)

time: 1450 us -> 1520 us (1.048)
  waiting for transfers between devices: 873 us -> 924 us
  local copies, waits for them, and re-layouts: 50.9 us -> 66.3 us
    ppermute x0 -> x2, waiting for transfers between devices: none -> 168 us  [connect_thing_in(): ppermute(seen_now, 'tensor', tuple(((c, (c - w_next) % g_now) for c in ra...]
    all_gather x1 -> x0, waiting for transfers between devices: 116 us -> none  [on_device(): lax.all_gather(grad_second.astype(jnp.bfloat16), 'tensor', axis=0, tiled=...]
    unnamed x94 -> x104, local copies, waits for them, and re-layouts: 20.2 us -> 32.2 us
    unnamed x15 -> x14, waiting for transfers between devices: 116 us -> 116 us
  transfers between devices with their start and end apart: 11 -> 12, of which waited for: 9 -> 10; matrix products, arithmetic and copies ran while one was open for 16% -> 16% of each run, Pallas kernels for 0% -> 0%
where the time goes in v1:
time: 1520 us
  waiting for transfers between devices  924 us (61%)
  matrix products  294 us (19%)
  other arithmetic  123 us (8%)
  local copies, waits for them, and re-layouts  66.3 us (4%)
  blocking collectives  55.5 us (4%)
  loops' own time  32.2 us (2%)
    psum x1, waiting for transfers between devices, on_device(): lax.psum(product(context, output_weight).astype(jnp.bfloat16), 'tensor')  226 us
    psum x1, waiting for transfers between devices, on_device(): lax.psum(lax.dynamic_update_slice_in_dim(up_back, mine_rows, part_id * sh...  224 us
    ppermute x2, waiting for transfers between devices, connect_thing_in(): ppermute(seen_now, 'tensor', tuple(((c, (c - w_next) % g_now) for c in ra...  168 us
    unnamed x14, waiting for transfers between devices  116 us
    reduce_scatter x1, waiting for transfers between devices, on_device(): lax.psum_scatter(product(hidden_low, down_weight).astype(jnp.bfloat16), '...  110 us
    dot_general x6, matrix products, contract_last(): lax.dot_general(left_side, right_side, (((1,), (1,)), ((), ())), preferre...  58.4 us
    reduce_scatter x1, waiting for transfers between devices, on_device(): lax.psum_scatter(grad_down_weight, 'dp', scatter_dimension=1, tiled=True)  45.1 us
    unnamed x1, blocking collectives  41.2 us
  transfers between devices with their start and end apart: 12, of which 10 were waited for; matrix products, arithmetic and copies ran while one was open for 16% of the time, Pallas kernels for 0%

profile of v1, /device:TPU:0, one launch (start us, length us, event | category | flops | bytes accessed | tf_op | source)
XLA Modules:
  0.0 1516.5 jit_solution(6222977816128036728)
XLA Ops:
  33.0 86.0 %while.26 = (s32[]{:T(128)}, bf16[8,512,3,64]{1,3,2,0:T(8,128)(2,1)}, f32[8,3,512]{2,1,0:T(4,128)S(1)}, s32[8]{0:T(128)S(1)}, bf16[4,1024,3,64]{1,3,2,0:T(8,128)...) while((s32[]{:T(128)}, ...), condition=%wide.region_3.4_spmd, body=%wide.region_0.3_spmd.sunk | while | flops 422148608 | bytes 22225096 | solution.py:75
  128.3 225.7 %all-reduce.11.cloned.1.call-done = bf16[4096,768]{1,0:T(8,128)(2,1)} async-done(((bf16[4096,768]{1,0:T(8,128)(2,1)}), bf16[4096,768]{1,0:T(8,128)(2,1)}) %all-reduce.11.cloned.1.call-update) | async-done | bytes 6291472 | tf_op jit(solution)/shard_map/psum | solution.py:185
  384.4 9.8 convolution_convert_fusion.1
  394.3 109.8 %reduce-scatter.17.cloned.1.call-done = bf16[1024,768]{1,0:T(8,128)(2,1)} async-done(((bf16[4096,768]{1,0:T(8,128)(2,1)}), bf16[1024,768]{1,0:T(8,128)(2,1)}) %reduce-scatter.17.cloned.1.call-update) | async-done | bytes 1572880 | tf_op jit(solution)/shard_map/reduce_scatter | solution.py:195
  520.8 33.8 %collective-permute-done = bf16[1024,768]{1,0:T(8,128)(2,1)S(1)} collective-permute-done((bf16[1024,768]{1,0:T(8,128)(2,1)S(1)}, bf16[1024,768]{1,0:T(8,128)(2,1)S(1)}, u32[]{:S(2)}, u32[]{:S(2)}) %collective-permute-start) | collective-permute-done | bytes 1572896 | tf_op jit(solution)/shard_map/ppermute | solution.py:162
  560.5 133.9 %collective-permute-done.1 = bf16[2048,768]{1,0:T(8,128)(2,1)} collective-permute-done((bf16[2048,768]{1,0:T(8,128)(2,1)}, bf16[2048,768]{1,0:T(8,128)(2,1)}, u32[]{:S(2)}, u32[]{:S(2)}) %collective-permute-start.1) | collective-permute-done | bytes 3145760 | tf_op jit(solution)/shard_map/ppermute | solution.py:162
  704.3 17.0 %convert_reduce_fusion = (f32[768]{0:T(1024)}, bf16[4096,768]{1,0:T(8,128)(2,1)S(1)}) fusion(f32[4096,768]{1,0:T(8,128)} %copy-done.38, f32[768]{0:T(1024)S(1)} %copy-done.35, bf16[768,768]{1,0:T(8,128)(2,1)S(1)} %copy-done, bf16[8192,768]{1,0:T(8,128)(2,1)} %constant_dynamic-update-slice_fusion, s32[]{:T(128)S(6)} %select_n.51), kind=kOutput, calls=%fused_computation.74 | convolution fusion | flops 4904188928 | bytes 26351620 | tf_op jit(solution)/shard_map/dot_general | solution.py:22
  721.3 8.0 fusion.91
  733.5 7.9 convert_element_type.120
  741.7 223.8 %all-reduce.13.cloned.1.call-done = bf16[4096,768]{1,0:T(8,128)(2,1)} async-done(((bf16[4096,768]{1,0:T(8,128)(2,1)}), bf16[4096,768]{1,0:T(8,128)(2,1)}) %all-reduce.13.cloned.1.call-update) | async-done | bytes 6291472 | tf_op jit(solution)/shard_map/psum | solution.py:217
  965.5 8.8 multiply_reduce_fusion.3
  990.1 7.9 convolution_convert_fusion.2
  1002.1 147.3 %while.27 = (s32[]{:T(128)}, bf16[8,512,3,64]{1,3,2,0:T(8,128)(2,1)}, f32[8,1024,3,64]{1,3,2,0:T(8,128)}, f32[8,1024,3,64]{1,3,2,0:T(8,128)}, s32[8]{0:T(128)S(1...) while((s32[]{:T(128)}, ...), condition=%wide.region_17.18_spmd, body=%wide.region_15.17_spmd.sunk | while | flops 1031043584 | bytes 53278952 | solution.py:115
  1176.6 12.8 add_convert_fusion
  1189.4 11.4 fusion.78
  1201.0 14.4 fusion.62
  1235.2 8.3 convert_element_type.121
  1243.8 14.3 all-reduce.7
  1263.1 36.2 %reduce-scatter.19.cloned.1.call-done = bf16[1024,768]{1,0:T(8,128)(2,1)} async-done(((bf16[4096,768]{1,0:T(8,128)(2,1)}), bf16[1024,768]{1,0:T(8,128)(2,1)}) %reduce-scatter.19.cloned.1.call-update) | async-done | bytes 1572880 | tf_op jit(solution)/shard_map/reduce_scatter | solution.py:247
  1303.6 41.2 %all-reduce.6 = (f32[768]{0:T(1024)S(1)}, f32[768]{0:T(1024)S(1)}, f32[768]{0:T(1024)S(1)}, f32[768]{0:T(1024)S(1)}, f32[768]{0:T(1024)S(1)}, /*index=5*/f32[768]{0:T(1024)S(1)}) all-reduce(f32[768]{0:T(1024)S(1)} %get-tuple-element.359, f32[768]{0:T(1024)S(1)} %get-tuple-element.287, ...), channel_id=8, replica_groups=mesh['dp'=8,'tensor'=4] {'dp','tensor'}, use_global_device_ids=true, to_apply=%region_30.31.clone | all-reduce | flops 4608 | bytes 36864
  1348.3 45.1 %reduce-scatter.23.cloned.1.call-done = f32[768,96]{0,1:T(8,128)} async-done(((f32[768,768]{0,1:T(8,128)}), f32[768,96]{0,1:T(8,128)}) %reduce-scatter.23.cloned.1.call-update) | async-done | bytes 294928 | tf_op jit(solution)/shard_map/reduce_scatter | solution.py:261
  1393.4 38.7 %reduce-scatter.25.cloned.1.call-done = f32[96,192]{1,0:T(8,128)} async-done(((f32[768,192]{1,0:T(8,128)}), f32[96,192]{1,0:T(8,128)}) %reduce-scatter.25.cloned.1.call-update) | async-done | bytes 73744
  1432.1 38.8 %reduce-scatter.27.cloned.1.call-done = f32[96,192]{1,0:T(8,128)} async-done(((f32[768,192]{1,0:T(8,128)}), f32[96,192]{1,0:T(8,128)}) %reduce-scatter.27.cloned.1.call-update) | async-done | bytes 73744
  1470.8 38.6 %reduce-scatter.29.cloned.1.call-done = f32[96,192]{1,0:T(8,128)} async-done(((f32[768,192]{1,0:T(8,128)}), f32[96,192]{1,0:T(8,128)}) %reduce-scatter.29.cloned.1.call-update) | async-done | bytes 73744
  (336 shorter events, 383.2 us)
Async XLA Ops:
  7.2 377.3 %copy-start = (bf16[768,768]{1,0:T(8,128)(2,1)S(1)}, bf16[768,768]{1,0:T(8,128)(2,1)}, u32[]{:S(2)}) copy-start(bf16[768,768]{1,0:T(8,128)(2,1)} %param.35) | copy-start | bytes 3538948
  7.2 346.7 %all-reduce.11.cloned.1.call-start = ((), (), s32[]{:S(2)}) async-start(), calls=%async_computation.8 | async-start | bytes 12582912 | tf_op jit(solution)/shard_map/psum | solution.py:185
  123.6 230.3 %copy-start.24 = (f32[768]{0:T(1024)S(1)}, f32[768]{0:T(1024)}, u32[]{:S(2)}) copy-start(f32[768]{0:T(1024)} %param.30) | copy-start | bytes 9220
  128.2 375.9 %reduce-scatter.17.cloned.1.call-start = ((), (), s32[]{:S(2)}) async-start(), calls=%async_computation.9 | async-start | bytes 7864320 | tf_op jit(solution)/shard_map/reduce_scatter | solution.py:195
  394.2 109.9 %copy-start.32 = (f32[768]{0:T(1024)S(1)}, f32[768]{0:T(1024)}, u32[]{:S(2)}) copy-start(f32[768]{0:T(1024)} %param.36) | copy-start | bytes 9220
  394.3 113.2 %copy-start.27 = (f32[768]{0:T(1024)S(1)}, f32[768]{0:T(1024)}, u32[]{:S(2)}) copy-start(f32[768]{0:T(1024)} %param.37) | copy-start | bytes 9220
  394.3 571.2 %all-reduce.13.cloned.1.call-start = ((), (), s32[]{:S(2)}) async-start(), calls=%async_computation.10 | async-start | bytes 12582912 | tf_op jit(solution)/shard_map/psum | solution.py:217
  394.3 116.9 %copy-start.30 = (f32[768]{0:T(1024)S(1)}, f32[768]{0:T(1024)}, u32[]{:S(2)}) copy-start(f32[768]{0:T(1024)} %param.38) | copy-start | bytes 9220
  518.2 36.4 %copy-start.12 = (bf16[1024,768]{1,0:T(8,128)(2,1)}, bf16[1024,768]{1,0:T(8,128)(2,1)S(1)}, u32[]{:S(2)}) copy-start(bf16[1024,768]{1,0:T(8,128)(2,1)S(1)} %get-tuple-element.350) | copy-start | bytes 4718596
  518.2 36.4 %collective-permute-start = (bf16[1024,768]{1,0:T(8,128)(2,1)S(1)}, bf16[1024,768]{1,0:T(8,128)(2,1)S(1)}, u32[]{:S(2)}, u32[]{:S(2)}) collective-permute-start(bf16[1024,768]{1,0:T(8,128)(2,1)S(1)} %get-tuple-element.350), channel_id=1, source_target_pairs={{0,3},{1,0},{2,1},{3,2},{4,7},{5,4},{6,5},{7,6},{8,11},{9,8},{10,9... | collective-permute-start | bytes 4718600 | tf_op jit(solution)/shard_map/ppermute | solution.py:162
  556.5 137.8 %collective-permute-start.1 = (bf16[2048,768]{1,0:T(8,128)(2,1)}, bf16[2048,768]{1,0:T(8,128)(2,1)}, u32[]{:S(2)}, u32[]{:S(2)}) collective-permute-start(bf16[2048,768]{1,0:T(8,128)(2,1)} %pad_maximum_fusion), channel_id=1, source_target_pairs={{0,2},{1,3},{2,0},{3,1},{4,6},{5,7},{6,4},{7,5},{8,10},{9,11},{10,... | collective-permute-start | bytes 9437192 | tf_op jit(solution)/shard_map/ppermute | solution.py:162
  559.2 138.9 %copy-start.13 = (bf16[1024,768]{1,0:T(8,128)(2,1)S(1)}, bf16[1024,768]{1,0:T(8,128)(2,1)}, u32[]{:S(2)}) copy-start(bf16[1024,768]{1,0:T(8,128)(2,1)} %copy-done.12) | copy-start | bytes 4718596
  704.3 17.0 %copy-start.34 = (bf16[768,768]{1,0:T(8,128)(2,1)S(1)}, bf16[768,768]{1,0:T(8,128)(2,1)}, u32[]{:S(2)}) copy-start(bf16[768,768]{1,0:T(8,128)(2,1)} %param.33) | copy-start | bytes 3538948
  741.4 520.0 %reduce-scatter.31.cloned.1.call-start = ((), (), s32[]{:S(2)}) async-start(), calls=%async_computation.17 | async-start | bytes 884736
  998.0 301.2 %reduce-scatter.19.cloned.1.call-start = ((), (), s32[]{:S(2)}) async-start(), calls=%async_computation.11 | async-start | bytes 7864320 | tf_op jit(solution)/shard_map/reduce_scatter | solution.py:247
  1189.4 158.9 %reduce-scatter.21.cloned.1.call-start = ((), (), s32[]{:S(2)}) async-start(), calls=%async_computation.12 | async-start | bytes 2654208 | tf_op jit(solution)/shard_map/reduce_scatter | solution.py:259
  1200.9 192.5 %reduce-scatter.23.cloned.1.call-start = ((), (), s32[]{:S(2)}) async-start(), calls=%async_computation.13 | async-start | bytes 2654208 | tf_op jit(solution)/shard_map/reduce_scatter | solution.py:261
  1215.4 216.7 %reduce-scatter.25.cloned.1.call-start = ((), (), s32[]{:S(2)}) async-start(), calls=%async_computation.14 | async-start | bytes 884736
  1221.3 249.6 %reduce-scatter.27.cloned.1.call-start = ((), (), s32[]{:S(2)}) async-start(), calls=%async_computation.15 | async-start | bytes 884736
  1227.3 282.1 %reduce-scatter.29.cloned.1.call-start = ((), (), s32[]{:S(2)}) async-start(), calls=%async_computation.16 | async-start | bytes 884736
  1243.8 265.6 %copy-start.1 = (bf16[768,768]{1,0:T(8,128)(2,1)S(1)}, bf16[768,768]{1,0:T(8,128)(2,1)}, u32[]{:S(2)}) copy-start(bf16[768,768]{1,0:T(8,128)(2,1)} %param.35) | copy-start | bytes 3538948
  1258.2 45.4 %copy-start.26 = (f32[768]{0:T(1024)S(1)}, f32[768]{0:T(1024)}, u32[]{:S(2)}) copy-start(f32[768]{0:T(1024)} %get-tuple-element.345) | copy-start | bytes 9220
  1258.2 45.4 %copy-start.28 = (f32[768]{0:T(1024)S(1)}, f32[768]{0:T(1024)}, u32[]{:S(2)}) copy-start(f32[768]{0:T(1024)} %get-tuple-element.288) | copy-start | bytes 9220
  1258.2 45.4 %copy-start.29 = (f32[768]{0:T(1024)S(1)}, f32[768]{0:T(1024)}, u32[]{:S(2)}) copy-start(f32[768]{0:T(1024)} %get-tuple-element.293) | copy-start | bytes 9220
  (31 other events, 226.9 us)
Sparse Core Ops, SparseCore 0:
  128.3 225.5 all-reduce.10
  394.4 109.6 reduce-scatter.16
  741.6 223.8 all-reduce.12
  998.1 33.9 reduce-scatter.30
  1189.5 109.7 reduce-scatter.18
  1303.0 43.4 reduce-scatter.20
  1350.8 42.4 reduce-scatter.22
  1397.1 34.9 reduce-scatter.24
  1435.8 34.9 reduce-scatter.26
  1474.4 34.9 reduce-scatter.28
